TPU v7x, 256 devices: a whole 4x4x8 slice. The times are simulated.
256 devices in a mesh: px: 4 (over z_lo), py: 8 (over y, core), ch: 8 (over z_hi, x).
Axes of the slice: x: 4, y: 4, z: 8 (z_hi: 2, z_lo: 4; z = z_hi * 4 + z_lo), core: 2. Of those that a mesh axis runs over, the one named last changes fastest.
Arguments:
- features: bfloat16 [128, 12, 8, 4, 512], P('ch', None, 'py', 'px'), may hold values from -6 to 6
- cotangent: bfloat16 [128, 12, 8, 4, 512], P('ch', None, 'py', 'px'), may hold values from -6 to 6
- weight: bfloat16 [3, 3, 128, 128], replicated, may hold values from -0.1875 to 0.1875
- edge_table: int32 [12, 4, 3], replicated, may hold values from 0 to 11, as said below
- corner_table: int32 [12, 4, 2], replicated, may hold values from 0 to 11, as said below
Outputs:
- activation: bfloat16 [128, 12, 8, 4, 512], P('ch', None, 'py', 'px')
- input_grad: bfloat16 [128, 12, 8, 4, 512], P('ch', None, 'py', 'px')
Inputs may be any that keep to these rules, and one draw needn't show every extreme that they name: edge_table[f, e] = (g, s, r): beyond edge e of face f lie the pixels of side s of face g, in reverse order if r = 1; every side of every face is named exactly once, and if (f, e) names (g, s) then (g, s) names (f, e) with the same r. corner_table[f, c] = (h, q): corner c of face f takes corner pixel q of face h; in each corner column every face appears once, and each q appears 12 times.
All inputs are finite; a program needn't handle non-finite values.
Results may differ from a plain program's by a relative error of at most 0.0049.
Values may be sent and summed in bfloat16 or wider, within the bound.
A program may use at most 192 MiB of HBM per device.

v0:
```python
import jax
import jax.numpy as jnp
from jax import lax
from jax.sharding import PartitionSpec as P

RB = 32


def with_halo(array, sides, width):
    for axis, dim in sides:
        size, length = (lax.axis_size(axis), array.shape[dim])
        up = [(i, (i + 1) % size) for i in range(size - 1)]
        down = [(j, i) for i, j in up]
        last = lax.slice_in_dim(array, length - width, length, axis=dim)
        leading = lax.slice_in_dim(array, 0, width, axis=dim)
        before = lax.ppermute(last, axis, up)
        after = lax.ppermute(leading, axis, down)
        array = jnp.concatenate([before, array, after], axis=dim)
    return array


def edge_strips(lines, edge_table, corner_table):
    chan_count = lines.shape[0]
    face_count = lines.shape[1]
    side_len = lines.shape[3]
    flat_lines = lines.reshape(chan_count, face_count * 4, side_len)
    pixels = jnp.stack(
        [lines[:, :, 0, 0], lines[:, :, 0, -1], lines[:, :, 1, 0], lines[:, :, 1, -1]], axis=2
    ).reshape(chan_count, face_count * 4)
    corner_index = corner_table[:, :, 0] * 4 + corner_table[:, :, 1]
    corner_vals = jnp.take(pixels, corner_index, axis=1)
    strips = []
    for edge_num, start_corner, end_corner in ((0, 0, 1), (1, 2, 3), (2, 0, 2), (3, 1, 3)):
        source_row = edge_table[:, edge_num, 0] * 4 + edge_table[:, edge_num, 1]
        strip_line = jnp.take(flat_lines, source_row, axis=1)
        flipped = (edge_table[:, edge_num, 2] == 1)[None, :, None]
        strip_line = jnp.where(flipped, strip_line[:, :, ::-1], strip_line)
        strips.append(
            jnp.concatenate(
                [
                    corner_vals[:, :, start_corner : start_corner + 1],
                    strip_line,
                    corner_vals[:, :, end_corner : end_corner + 1],
                ],
                axis=2,
            )
        )
    return strips


def face_lines_of(field, row_pos, col_pos, px_count, py_count):
    chan_block = field.shape[0]
    face_count = field.shape[1]
    col_len = field.shape[2]
    row_len = field.shape[3]
    side_len = row_len * px_count
    blank = jnp.zeros((chan_block, face_count, side_len), jnp.float32)

    def placed(values, offset, active):
        return jnp.where(
            active,
            lax.dynamic_update_slice_in_dim(blank, values.astype(jnp.float32), offset, 2),
            0.0,
        )

    contrib = jnp.stack(
        [
            placed(field[:, :, 0, :], row_pos * row_len, col_pos == 0),
            placed(field[:, :, -1, :], row_pos * row_len, col_pos == py_count - 1),
            placed(field[:, :, :, 0], col_pos * col_len, row_pos == 0),
            placed(field[:, :, :, -1], col_pos * col_len, row_pos == px_count - 1),
        ],
        axis=2,
    )
    return lax.psum(contrib.astype(jnp.bfloat16), ("px", "py"))


def pad_field(field, edge_table, corner_table):
    col_len = field.shape[2]
    row_len = field.shape[3]
    row_pos = lax.axis_index("px")
    col_pos = lax.axis_index("py")
    px_count = lax.axis_size("px")
    py_count = lax.axis_size("py")
    padded = with_halo(field, (("px", 3), ("py", 2)), 1)
    lines = face_lines_of(field, row_pos, col_pos, px_count, py_count)
    strips = edge_strips(lines, edge_table, corner_table)
    top_row = lax.dynamic_slice_in_dim(strips[0], row_pos * row_len, row_len + 2, 2)
    bottom_row = lax.dynamic_slice_in_dim(strips[1], row_pos * row_len, row_len + 2, 2)
    left_col = lax.dynamic_slice_in_dim(strips[2], col_pos * col_len, col_len + 2, 2)
    right_col = lax.dynamic_slice_in_dim(strips[3], col_pos * col_len, col_len + 2, 2)
    padded = padded.at[:, :, 0, :].set(jnp.where(col_pos == 0, top_row, padded[:, :, 0, :]))
    padded = padded.at[:, :, -1, :].set(
        jnp.where(col_pos == py_count - 1, bottom_row, padded[:, :, -1, :])
    )
    padded = padded.at[:, :, :, 0].set(jnp.where(row_pos == 0, left_col, padded[:, :, :, 0]))
    padded = padded.at[:, :, :, -1].set(
        jnp.where(row_pos == px_count - 1, right_col, padded[:, :, :, -1])
    )
    return padded


def forward_taps(padded, taps, out_cols, out_rows):
    summed = None
    for tap_row in range(3):
        for tap_col in range(3):
            window = padded[:, :, tap_row : tap_row + out_cols, tap_col : tap_col + out_rows]
            term_val = jnp.einsum(
                "oc,cfab->ofab", taps[tap_row, tap_col], window, preferred_element_type=jnp.float32
            )
            summed = term_val if summed is None else summed + term_val
    return summed


def backward_taps(padded, taps, out_cols, out_rows):
    summed = None
    for tap_row in range(3):
        for tap_col in range(3):
            window = padded[
                :, :, 2 - tap_row : 2 - tap_row + out_cols, 2 - tap_col : 2 - tap_col + out_rows
            ]
            term_val = jnp.einsum(
                "oc,ofab->cfab", taps[tap_row, tap_col], window, preferred_element_type=jnp.float32
            )
            summed = term_val if summed is None else summed + term_val
    return summed


def gate_outputs(preact, cotangent):
    sigmoid_val = jax.nn.sigmoid(preact)
    activation = (preact * sigmoid_val).astype(jnp.bfloat16)
    gated = (
        cotangent.astype(jnp.float32) * sigmoid_val * (1.0 + preact * (1.0 - sigmoid_val))
    ).astype(jnp.bfloat16)
    return (activation, gated)


def local(features, cotangent, weight, edge_table, corner_table):
    chan_block = features.shape[0]
    face_count = features.shape[1]
    tile_len = features.shape[4]
    row_len = RB
    col_len = tile_len // row_len
    features = features.reshape(chan_block, face_count, col_len, row_len)
    cotangent = cotangent.reshape(chan_block, face_count, col_len, row_len)
    ch_pos = lax.axis_index("ch")
    feat_pad = pad_field(features, edge_table, corner_table)
    own_taps = lax.dynamic_slice_in_dim(weight, ch_pos * chan_block, chan_block, 2)
    piece_taps = own_taps
    preact = forward_taps(
        lax.all_gather(feat_pad, "ch", axis=0, tiled=True), piece_taps, col_len, row_len
    )
    activation, gated = gate_outputs(preact, cotangent)
    grad_pad = pad_field(gated, edge_table, corner_table)
    input_taps = lax.dynamic_slice_in_dim(weight, ch_pos * chan_block, chan_block, 3)
    piece_taps = input_taps
    input_grad = backward_taps(
        lax.all_gather(grad_pad, "ch", axis=0, tiled=True), piece_taps, col_len, row_len
    ).astype(jnp.bfloat16)
    out_shape = (chan_block, face_count, 1, 1, tile_len)
    return (activation.reshape(out_shape), input_grad.reshape(out_shape))


def solution(mesh):
    return jax.shard_map(
        local,
        mesh=mesh,
        in_specs=(P("ch", None, "py", "px", None), P("ch", None, "py", "px", None), P(), P(), P()),
        out_specs=(P("ch", None, "py", "px", None), P("ch", None, "py", "px", None)),
        check_vma=False,
    )
```

profile of v0, /device:TPU:8, one launch (start us, length us, event | category | flops | bytes accessed | tf_op | source)
XLA Modules:
  0.0 1055.1 jit_solution(10775510683861696942)
XLA Ops:
  11.2 3.0 copy.696
  16.1 2.7 select_n.196
  18.7 2.7 select_n.200
  23.1 2.6 copy.698
  27.0 7.1 collective-permute-start
  43.6 1.9 collective-permute-start.2
  45.5 3.9 collective-permute-start.3
  53.1 254.8 %all-reduce.3.cloned.1.call-done = bf16[16,12,4,128]{1,0,3,2:T(8,128)(2,1)} async-done(((bf16[16,12,4,128]{1,0,3,2:T(8,128)(2,1)}), bf16[16,12,4,128]{1,0,3,2:T(8,128)(2,1)}) %all-reduce.3.cloned.1.call-update) | async-done | bytes 196624 | tf_op jit(solution)/shard_map/psum | solution.py:75
  307.9 3.0 copy.702
  318.9 3.8 scatter.30
  326.8 18.3 %scatter.31 = bf16[16,12,18,34]{3,0,2,1:T(8,128)(2,1)S(1)} dynamic-update-slice(bf16[16,12,18,34]{3,0,2,1:T(8,128)(2,1)S(1)} %scatter.30, bf16[16,12,18,1]{3,0,2,1:T(8,128)(2,1)S(1)} %copy.707, s32[]{:T(128)} %constant.235.clone.1, s32[]{:T(128)} %constant.235.clone.1, s32[]{:T(128)} %constant.235.clone.1, s32[]{:T(128)} %constant.249.clone.1) | dynamic-update-slice | bytes 13828 | tf_op jit(solution)/shard_map/scatter | solution.py:97
  347.9 162.8 %all-gather.3.cloned.1.call-done = bf16[128,12,18,34]{3,0,2,1:T(8,128)(2,1)} async-done(((bf16[16,12,18,34]{3,0,2,1:T(8,128)(2,1)}), bf16[128,12,18,34]{3,0,2,1:T(8,128)(2,1)}) %all-gather.3.cloned.1.call-update) | async-done | bytes 1880080 | tf_op jit(solution)/shard_map/all_gather | solution.py:151
  510.7 4.7 fusion.20
  524.6 2.0 fusion.18
  526.6 2.6 fusion.37
  531.6 2.3 copy.725
  536.3 2.2 collective-permute-start.4
  541.1 1.9 select_n.220
  543.0 1.9 select_n.223
  545.7 2.6 copy.727
  551.1 1.9 collective-permute-start.6
  553.0 3.9 collective-permute-start.7
  559.2 266.2 %all-reduce.5.cloned.1.call-done = bf16[16,12,4,128]{1,0,3,2:T(8,128)(2,1)} async-done(((bf16[16,12,4,128]{1,0,3,2:T(8,128)(2,1)}), bf16[16,12,4,128]{1,0,3,2:T(8,128)(2,1)}) %all-reduce.5.cloned.1.call-update) | async-done | bytes 196624 | tf_op jit(solution)/shard_map/psum | solution.py:75
  825.4 3.0 copy.731
  837.1 3.8 scatter.36
  844.2 18.6 %scatter.39 = bf16[16,12,18,34]{3,0,2,1:T(8,128)(2,1)S(1)} dynamic-update-slice(bf16[16,12,18,34]{3,0,2,1:T(8,128)(2,1)S(1)} %scatter.36, bf16[16,12,18,1]{3,0,2,1:T(8,128)(2,1)S(1)} %copy.735, s32[]{:T(128)} %constant.235.clone.1, s32[]{:T(128)} %constant.235.clone.1, s32[]{:T(128)} %constant.235.clone.1, s32[]{:T(128)} %constant.249.clone.1) | dynamic-update-slice | bytes 13828 | tf_op jit(solution)/shard_map/scatter | solution.py:97
  865.5 162.9 %all-gather.5.cloned.1.call-done = bf16[128,12,18,34]{3,0,2,1:T(8,128)(2,1)} async-done(((bf16[16,12,18,34]{3,0,2,1:T(8,128)(2,1)}), bf16[128,12,18,34]{3,0,2,1:T(8,128)(2,1)}) %all-gather.5.cloned.1.call-update) | async-done | bytes 1880080 | tf_op jit(solution)/shard_map/all_gather | solution.py:158
  1028.4 4.8 fusion.2
  1034.3 1.9 fusion.10
  1037.2 1.9 fusion.14
  1040.9 1.9 fusion.8
  1044.1 2.3 add_convert_fusion
  (201 shorter events, 80.0 us)
Async XLA Ops:
  7.2 503.6 %copy-start = (bf16[3,3,128,128]{3,2,1,0:T(8,128)(2,1)S(1)}, bf16[3,3,128,128]{3,2,1,0:T(8,128)(2,1)}, u32[]{:S(2)}) copy-start(bf16[3,3,128,128]{3,2,1,0:T(8,128)(2,1)} %param.27) | copy-start | bytes 884740
  7.2 300.8 %all-reduce.3.cloned.1.call-start = ((), (), s32[]{:S(2)}) async-start(), calls=%async_computation | async-start | bytes 4194304 | tf_op jit(solution)/shard_map/psum | solution.py:75
  25.7 10.9 %copy-start.17 = (s32[12,4,3]{0,1,2:T(4,128)S(1)}, s32[12,4,3]{0,1,2:T(4,128)}, u32[]{:S(2)}) copy-start(s32[12,4,3]{0,1,2:T(4,128)} %param.28) | copy-start | bytes 1732
  25.7 12.0 %copy-start.26 = (s32[12,4,2]{0,2,1:T(2,128)S(1)}, s32[12,4,2]{0,2,1:T(2,128)}, u32[]{:S(2)}) copy-start(s32[12,4,2]{0,2,1:T(2,128)} %param.29) | copy-start | bytes 1156
  25.7 485.0 %all-gather.3.cloned.1.call-start = ((), (), s32[]{:S(2)}) async-start(), calls=%async_computation.1 | async-start | bytes 7962624 | tf_op jit(solution)/shard_map/all_gather | solution.py:151
  27.0 12.3 %collective-permute-start = (bf16[16,12,16,1]{2,0,3,1:T(8,128)(2,1)S(1)}, bf16[16,12,16,1]{2,0,3,1:T(8,128)(2,1)S(1)}, u32[]{:S(2)}, u32[]{:S(2)}) collective-permute-start(bf16[16,12,16,1]{2,0,3,1:T(8,128)(2,1)S(1)} %copy.684), channel_id=1, source_target_pairs={{0,64},{64,128},{128,192},{1,65},{65,129},{129,193},{2,66},{66,130... | collective-permute-start | bytes 18440 | tf_op jit(solution)/shard_map/ppermute | solution.py:16
  35.3 6.0 collective-permute-start.1
  43.6 5.9 collective-permute-start.2
  45.5 5.4 collective-permute-start.3
  53.1 258.7 %copy-start.15 = (pred[12]{0:T(512)(128)(4,1)S(1)}, pred[12]{0:T(512)(128)(4,1)}, u32[]{:S(2)}) copy-start(pred[12]{0:T(512)(128)(4,1)} %get-tuple-element.166) | copy-start | bytes 40
  53.1 259.6 %copy-start.13 = (pred[12]{0:T(512)(128)(4,1)S(1)}, pred[12]{0:T(512)(128)(4,1)}, u32[]{:S(2)}) copy-start(pred[12]{0:T(512)(128)(4,1)} %get-tuple-element.164) | copy-start | bytes 40
  311.0 4.6 copy-start.20
  311.0 4.7 copy-start.11
  311.0 4.9 copy-start.22
  313.8 3.6 copy-start.24
  346.1 479.3 %all-reduce.5.cloned.1.call-start = ((), (), s32[]{:S(2)}) async-start(), calls=%async_computation.2 | async-start | bytes 4194304 | tf_op jit(solution)/shard_map/psum | solution.py:75
  510.7 4.8 copy-start.2
  535.1 9.9 copy-start.7
  535.1 10.2 copy-start.6
  536.3 12.1 %collective-permute-start.4 = (bf16[16,12,16,1]{2,0,3,1:T(8,128)(2,1)S(1)}, bf16[16,12,16,1]{2,0,3,1:T(8,128)(2,1)S(1)}, u32[]{:S(2)}, u32[]{:S(2)}) collective-permute-start(bf16[16,12,16,1]{2,0,3,1:T(8,128)(2,1)S(1)} %copy.720), channel_id=1, source_target_pairs={{0,64},{64,128},{128,192},{1,65},{65,129},{129,193},{2,66},{66,130... | collective-permute-start | bytes 18440 | tf_op jit(solution)/shard_map/ppermute | solution.py:16
  539.8 9.9 collective-permute-start.5
  548.4 480.1 %all-gather.5.cloned.1.call-start = ((), (), s32[]{:S(2)}) async-start(), calls=%async_computation.3 | async-start | bytes 7962624 | tf_op jit(solution)/shard_map/all_gather | solution.py:158
  551.1 5.8 collective-permute-start.6
  553.0 5.4 collective-permute-start.7
  559.1 272.2 %copy-start.16 = (pred[12]{0:T(512)(128)(4,1)S(1)}, pred[12]{0:T(512)(128)(4,1)}, u32[]{:S(2)}) copy-start(pred[12]{0:T(512)(128)(4,1)} %get-tuple-element.166) | copy-start | bytes 40
  559.2 272.4 %copy-start.25 = (pred[12]{0:T(512)(128)(4,1)S(1)}, pred[12]{0:T(512)(128)(4,1)}, u32[]{:S(2)}) copy-start(pred[12]{0:T(512)(128)(4,1)} %get-tuple-element.162) | copy-start | bytes 40
  559.2 272.5 %copy-start.14 = (pred[12]{0:T(512)(128)(4,1)S(1)}, pred[12]{0:T(512)(128)(4,1)}, u32[]{:S(2)}) copy-start(pred[12]{0:T(512)(128)(4,1)} %get-tuple-element.164) | copy-start | bytes 40
  559.2 272.7 %copy-start.23 = (pred[12]{0:T(512)(128)(4,1)S(1)}, pred[12]{0:T(512)(128)(4,1)}, u32[]{:S(2)}) copy-start(pred[12]{0:T(512)(128)(4,1)} %get-tuple-element.161) | copy-start | bytes 40
  828.4 5.5 copy-start.21
  828.5 5.6 copy-start.9
  842.9 20.9 %copy-start.5 = (bf16[16,12,16,32]{3,0,2,1:T(8,128)(2,1)S(1)}, bf16[16,12,16,32]{3,0,2,1:T(8,128)(2,1)}, u32[]{:S(2)}) copy-start(bf16[16,12,16,32]{3,0,2,1:T(8,128)(2,1)} %get-tuple-element.139) | copy-start | bytes 589828
  1028.4 4.8 copy-start.1
  (7 other events, 9.8 us)
Sparse Core Ops, SparseCore 0:
  25.8 282.0 all-reduce.2
  346.2 164.4 all-gather.2
  548.5 276.8 all-reduce.4
  863.9 164.4 all-gather.4
where the time goes:
time: 1060 us
  waiting for transfers between devices  850 us (80%)
  local copies, waits for them, and re-layouts  117 us (11%)
  matrix products  36.3 us (3%)
  starting transfers between devices  24 us (2%)
  between operations  15.2 us (1%)
  other arithmetic  12.9 us (1%)
    psum x2, waiting for transfers between devices, face_lines_of(): return lax.psum(contrib.astype(jnp.bfloat16), ('px', 'py'))  521 us
    all_gather x1, waiting for transfers between devices, local(): lax.all_gather(grad_pad, 'ch', axis=0, tiled=True)  163 us
    all_gather x1, waiting for transfers between devices, local(): lax.all_gather(feat_pad, 'ch', axis=0, tiled=True)  163 us
    scatter x2, local copies, waits for them, and re-layouts, pad_field(): padded.at[:, :, :, -1]  36.9 us
  transfers between devices with their start and end apart: 12, of which 7 were waited for; matrix products, arithmetic and copies ran while one was open for 2% of the time, Pallas kernels for 0%

commit v1 on v0

--- a/solution.py
+++ b/solution.py
@@ -155,7 +155,12 @@
     input_taps = lax.dynamic_slice_in_dim(weight, ch_pos * chan_block, chan_block, 3)
     piece_taps = input_taps
     input_grad = backward_taps(
-        lax.all_gather(grad_pad, "ch", axis=0, tiled=True), piece_taps, col_len, row_len
+        jnp.concatenate(
+            lax.all_to_all(jnp.stack([grad_pad] * lax.axis_size("ch")), "ch", 0, 0), axis=0
+        ),
+        piece_taps,
+        col_len,
+        row_len,
     ).astype(jnp.bfloat16)
     out_shape = (chan_block, face_count, 1, 1, tile_len)
     return (activation.reshape(out_shape), input_grad.reshape(out_shape))

time: 1060 us -> 985 us (0.929); the launches traced: 1060 us -> 967 us
  waiting for transfers between devices: 850 us -> 709 us
  local copies, waits for them, and re-layouts: 117 us -> 164 us
    all_gather x1 -> x0, waiting for transfers between devices: 163 us -> none  [local(): lax.all_gather(grad_pad, 'ch', axis=0, tiled=True)]
    unnamed x54 -> x51, local copies, waits for them, and re-layouts: 2.85 us -> 43.9 us
    all_to_all x0 -> x1, waiting for transfers between devices: none -> 21.7 us  [local(): lax.all_to_all(jnp.stack([grad_pad] * lax.axis_size('ch')), 'ch', 0, 0)]
    scatter x2 -> x3, local copies, waits for them, and re-layouts: 36.9 us -> 37.9 us  [pad_field(): padded.at[:, :, :, -1]]
  transfers between devices with their start and end apart: 12 -> 12, of which waited for: 7 -> 7; matrix products, arithmetic and copies ran while one was open for 2% -> 3% of each run, Pallas kernels for 0% -> 0%
where the time goes in v1:
time: 985 us; the launch traced here: 967 us
  waiting for transfers between devices  709 us (72%)
  local copies, waits for them, and re-layouts  164 us (17%)
  matrix products  33.7 us (3%)
  starting transfers between devices  33.1 us (3%)
  between operations  15.2 us (2%)
  other arithmetic  12.8 us (1%)
    psum x2, waiting for transfers between devices, face_lines_of(): return lax.psum(contrib.astype(jnp.bfloat16), ('px', 'py'))  521 us
    all_gather x1, waiting for transfers between devices, local(): lax.all_gather(feat_pad, 'ch', axis=0, tiled=True)  163 us
    unnamed x51, local copies, waits for them, and re-layouts  43.9 us
    scatter x3, local copies, waits for them, and re-layouts, pad_field(): padded.at[:, :, :, -1]  37.9 us
    all_to_all x1, waiting for transfers between devices, local(): lax.all_to_all(jnp.stack([grad_pad] * lax.axis_size('ch')), 'ch', 0, 0)  21.7 us
  transfers between devices with their start and end apart: 12, of which 7 were waited for; matrix products, arithmetic and copies ran while one was open for 3% of the time, Pallas kernels for 0%

profile of v1, /device:TPU:8, one launch (start us, length us, event | category | flops | bytes accessed | tf_op | source)
XLA Modules:
  0.0 967.1 jit_solution(11605734247841137968)
XLA Ops:
  11.2 3.0 copy.696
  16.0 2.7 select_n.196
  18.7 2.7 select_n.200
  23.0 2.6 copy.698
  26.9 7.1 collective-permute-start
  43.5 1.9 collective-permute-start.2
  45.5 4.2 collective-permute-start.3
  53.1 254.8 %all-reduce.3.cloned.1.call-done = bf16[16,12,4,128]{1,0,3,2:T(8,128)(2,1)} async-done(((bf16[16,12,4,128]{1,0,3,2:T(8,128)(2,1)}), bf16[16,12,4,128]{1,0,3,2:T(8,128)(2,1)}) %all-reduce.3.cloned.1.call-update) | async-done | bytes 196624 | tf_op jit(solution)/shard_map/psum | solution.py:75
  307.9 3.0 copy.702
  318.9 3.8 scatter.34
  326.7 18.3 %scatter.35 = bf16[16,12,18,34]{3,0,2,1:T(8,128)(2,1)S(1)} dynamic-update-slice(bf16[16,12,18,34]{3,0,2,1:T(8,128)(2,1)S(1)} %scatter.34, bf16[16,12,18,1]{3,0,2,1:T(8,128)(2,1)S(1)} %copy.707, s32[]{:T(128)} %constant.237.clone.1, s32[]{:T(128)} %constant.237.clone.1, s32[]{:T(128)} %constant.237.clone.1, s32[]{:T(128)} %constant.251.clone.1) | dynamic-update-slice | bytes 13828 | tf_op jit(solution)/shard_map/scatter | solution.py:97
  347.7 163.0 %all-gather.2.cloned.1.call-done = bf16[128,12,18,34]{3,0,2,1:T(8,128)(2,1)} async-done(((bf16[16,12,18,34]{3,0,2,1:T(8,128)(2,1)}), bf16[128,12,18,34]{3,0,2,1:T(8,128)(2,1)}) %all-gather.2.cloned.1.call-update) | async-done | bytes 1880080 | tf_op jit(solution)/shard_map/all_gather | solution.py:151
  510.7 4.7 fusion.20
  524.6 2.2 fusion.18
  526.8 2.5 fusion.37
  531.7 2.3 copy.725
  536.5 2.2 collective-permute-start.4
  541.2 1.9 select_n.220
  543.2 1.9 select_n.223
  545.8 2.6 copy.727
  553.1 3.8 collective-permute-start.7
  559.3 266.3 %all-reduce.5.cloned.1.call-done = bf16[16,12,4,128]{1,0,3,2:T(8,128)(2,1)} async-done(((bf16[16,12,4,128]{1,0,3,2:T(8,128)(2,1)}), bf16[16,12,4,128]{1,0,3,2:T(8,128)(2,1)}) %all-reduce.5.cloned.1.call-update) | async-done | bytes 196624 | tf_op jit(solution)/shard_map/psum | solution.py:75
  825.5 3.0 copy.731
  837.2 3.8 scatter.48
  844.3 18.3 %scatter.50 = bf16[16,12,18,34]{3,0,2,1:T(8,128)(2,1)S(1)} dynamic-update-slice(bf16[16,12,18,34]{3,0,2,1:T(8,128)(2,1)S(1)} %scatter.48, bf16[16,12,18,1]{3,0,2,1:T(8,128)(2,1)S(1)} %copy.735, s32[]{:T(128)} %constant.237.clone.1, s32[]{:T(128)} %constant.237.clone.1, s32[]{:T(128)} %constant.237.clone.1, s32[]{:T(128)} %constant.251.clone.1) | dynamic-update-slice | bytes 13828 | tf_op jit(solution)/shard_map/scatter | solution.py:97
  862.6 4.0 broadcast_bitcast_fusion
  866.7 15.8 %reshape.584 = bf16[8,2,58752]{2,1,0:T(2,128)(2,1)} reshape(bf16[8,12,18,16,34]{4,3,2,1,0:T(8,128)(2,1)} %broadcast_bitcast_fusion) | data formatting | bytes 3760128
  882.5 9.1 all-to-all-start
  894.4 21.7 %all-to-all-done = bf16[8,2,58752]{2,1,0:T(2,128)(2,1)S(1)} async-done(((bf16[8,2,58752]{2,1,0:T(2,128)(2,1)}), bf16[8,2,58752]{2,1,0:T(2,128)(2,1)S(1)}, u32[]{:S(2)}, u32[]{:S(2)}) %all-to-all-start) | async-done | bytes 1880096 | tf_op jit(solution)/shard_map/all_to_all | solution.py:159
  916.1 22.2 %reshape.585 = bf16[8,12,18,16,34]{4,3,2,1,0:T(8,128)(2,1)} reshape(bf16[8,2,58752]{2,1,0:T(2,128)(2,1)S(1)} %all-to-all-done) | data formatting | bytes 3760128
  938.3 5.1 copy.736
  956.1 2.4 add_convert_fusion
  (198 shorter events, 88.8 us)
Async XLA Ops:
  7.2 503.5 %copy-start = (bf16[3,3,128,128]{3,2,1,0:T(8,128)(2,1)S(1)}, bf16[3,3,128,128]{3,2,1,0:T(8,128)(2,1)}, u32[]{:S(2)}) copy-start(bf16[3,3,128,128]{3,2,1,0:T(8,128)(2,1)} %param.27) | copy-start | bytes 884740
  7.2 300.7 %all-reduce.3.cloned.1.call-start = ((), (), s32[]{:S(2)}) async-start(), calls=%async_computation.1 | async-start | bytes 4194304 | tf_op jit(solution)/shard_map/psum | solution.py:75
  25.7 10.9 %copy-start.14 = (s32[12,4,3]{0,1,2:T(4,128)S(1)}, s32[12,4,3]{0,1,2:T(4,128)}, u32[]{:S(2)}) copy-start(s32[12,4,3]{0,1,2:T(4,128)} %param.28) | copy-start | bytes 1732
  25.7 12.0 %copy-start.23 = (s32[12,4,2]{0,2,1:T(2,128)S(1)}, s32[12,4,2]{0,2,1:T(2,128)}, u32[]{:S(2)}) copy-start(s32[12,4,2]{0,2,1:T(2,128)} %param.29) | copy-start | bytes 1156
  25.7 485.0 %all-gather.2.cloned.1.call-start = ((), (), s32[]{:S(2)}) async-start(), calls=%async_computation.2 | async-start | bytes 7962624 | tf_op jit(solution)/shard_map/all_gather | solution.py:151
  26.9 12.4 %collective-permute-start = (bf16[16,12,16,1]{2,0,3,1:T(8,128)(2,1)S(1)}, bf16[16,12,16,1]{2,0,3,1:T(8,128)(2,1)S(1)}, u32[]{:S(2)}, u32[]{:S(2)}) collective-permute-start(bf16[16,12,16,1]{2,0,3,1:T(8,128)(2,1)S(1)} %copy.684), channel_id=1, source_target_pairs={{0,64},{64,128},{128,192},{1,65},{65,129},{129,193},{2,66},{66,130... | collective-permute-start | bytes 18440 | tf_op jit(solution)/shard_map/ppermute | solution.py:16
  35.2 6.0 collective-permute-start.1
  43.5 6.2 collective-permute-start.2
  45.5 5.4 collective-permute-start.3
  53.1 258.7 %copy-start.12 = (pred[12]{0:T(512)(128)(4,1)S(1)}, pred[12]{0:T(512)(128)(4,1)}, u32[]{:S(2)}) copy-start(pred[12]{0:T(512)(128)(4,1)} %get-tuple-element.166) | copy-start | bytes 40
  53.1 259.6 %copy-start.10 = (pred[12]{0:T(512)(128)(4,1)S(1)}, pred[12]{0:T(512)(128)(4,1)}, u32[]{:S(2)}) copy-start(pred[12]{0:T(512)(128)(4,1)} %get-tuple-element.164) | copy-start | bytes 40
  53.1 262.4 %copy-start.17 = (pred[12]{0:T(512)(128)(4,1)S(1)}, pred[12]{0:T(512)(128)(4,1)}, u32[]{:S(2)}) copy-start(pred[12]{0:T(512)(128)(4,1)} %get-tuple-element.163) | copy-start | bytes 40
  311.0 4.7 copy-start.8
  311.0 4.8 copy-start.19
  312.8 4.5 copy-start.21
  322.7 2.5 copy-start.15
  346.1 479.5 %all-reduce.5.cloned.1.call-start = ((), (), s32[]{:S(2)}) async-start(), calls=%async_computation.3 | async-start | bytes 4194304 | tf_op jit(solution)/shard_map/psum | solution.py:75
  510.7 4.8 copy-start.1
  535.3 9.9 %copy-start.4 = (bf16[16,12,1,32]{3,0,2,1:T(8,128)(2,1)S(1)}, bf16[16,12,1,32]{3,0,2,1:T(8,128)(2,1)}, u32[]{:S(2)}) copy-start(bf16[16,12,1,32]{3,0,2,1:T(8,128)(2,1)} %get-tuple-element.140) | copy-start | bytes 36868
  535.3 10.2 %copy-start.3 = (bf16[16,12,1,32]{3,0,2,1:T(8,128)(2,1)S(1)}, bf16[16,12,1,32]{3,0,2,1:T(8,128)(2,1)}, u32[]{:S(2)}) copy-start(bf16[16,12,1,32]{3,0,2,1:T(8,128)(2,1)} %get-tuple-element.141) | copy-start | bytes 36868
  536.5 12.0 %collective-permute-start.4 = (bf16[16,12,16,1]{2,0,3,1:T(8,128)(2,1)S(1)}, bf16[16,12,16,1]{2,0,3,1:T(8,128)(2,1)S(1)}, u32[]{:S(2)}, u32[]{:S(2)}) collective-permute-start(bf16[16,12,16,1]{2,0,3,1:T(8,128)(2,1)S(1)} %copy.720), channel_id=1, source_target_pairs={{0,64},{64,128},{128,192},{1,65},{65,129},{129,193},{2,66},{66,130... | collective-permute-start | bytes 18440 | tf_op jit(solution)/shard_map/ppermute | solution.py:16
  539.9 9.9 %collective-permute-start.5 = (bf16[16,12,16,1]{2,0,3,1:T(8,128)(2,1)S(1)}, bf16[16,12,16,1]{2,0,3,1:T(8,128)(2,1)S(1)}, u32[]{:S(2)}, u32[]{:S(2)}) collective-permute-start(bf16[16,12,16,1]{2,0,3,1:T(8,128)(2,1)S(1)} %copy.721), channel_id=1, source_target_pairs={{64,0},{128,64},{192,128},{65,1},{129,65},{193,129},{66,2},{130,66... | collective-permute-start | bytes 18440 | tf_op jit(solution)/shard_map/ppermute | solution.py:17
  551.2 5.8 collective-permute-start.6
  553.1 5.4 collective-permute-start.7
  559.2 272.3 %copy-start.13 = (pred[12]{0:T(512)(128)(4,1)S(1)}, pred[12]{0:T(512)(128)(4,1)}, u32[]{:S(2)}) copy-start(pred[12]{0:T(512)(128)(4,1)} %get-tuple-element.166) | copy-start | bytes 40
  559.2 272.5 %copy-start.22 = (pred[12]{0:T(512)(128)(4,1)S(1)}, pred[12]{0:T(512)(128)(4,1)}, u32[]{:S(2)}) copy-start(pred[12]{0:T(512)(128)(4,1)} %get-tuple-element.162) | copy-start | bytes 40
  559.3 272.6 %copy-start.11 = (pred[12]{0:T(512)(128)(4,1)S(1)}, pred[12]{0:T(512)(128)(4,1)}, u32[]{:S(2)}) copy-start(pred[12]{0:T(512)(128)(4,1)} %get-tuple-element.164) | copy-start | bytes 40
  559.3 272.7 %copy-start.20 = (pred[12]{0:T(512)(128)(4,1)S(1)}, pred[12]{0:T(512)(128)(4,1)}, u32[]{:S(2)}) copy-start(pred[12]{0:T(512)(128)(4,1)} %get-tuple-element.161) | copy-start | bytes 40
  828.6 5.5 copy-start.18
  828.6 5.6 copy-start.6
  841.0 1.8 copy-start.16
  882.5 33.6 %all-to-all-start = ((bf16[8,2,58752]{2,1,0:T(2,128)(2,1)}), bf16[8,2,58752]{2,1,0:T(2,128)(2,1)S(1)}, u32[]{:S(2)}, u32[]{:S(2)}) async-start(bf16[8,2,58752]{2,1,0:T(2,128)(2,1)} %reshape.584), calls=%async_computation | async-start | bytes 3760128 | tf_op jit(solution)/shard_map/all_to_all | solution.py:159
  (4 other events, 4.3 us)
Sparse Core Ops, SparseCore 0:
  25.8 282.0 all-reduce.2
  346.2 164.4 all-gather.1
  548.6 276.8 all-reduce.4
